TPU v7x, 32 devices: a whole 2x2x4 slice. The times are simulated.
32 devices in a mesh: row: 2 (over x), col: 8 (over z, y), layer: 2 (over core).
Axes of the slice: x: 2, y: 2, z: 4, core: 2. Of those that a mesh axis runs over, the one named last changes fastest.
Arguments:
- owned_blocks: bfloat16 [512, 32, 128, 128], P(('row', 'col', 'layer')), may hold values from -1 to 1
- slot_rows: int32 [512], P(('row', 'col', 'layer')), may hold values from -1 to 255, as said below
- block_cols: int32 [512, 32], P(('row', 'col', 'layer')), may hold values from 0 to 255, as said below
Outputs:
- product_blocks: bfloat16 [256, 32, 128, 128], P(('row', 'layer'), 'col')
Inputs may be any that keep to these rules, and one draw needn't show every extreme that they name: `slot_rows`: every block row appears in exactly one slot. The 16 slots of the device at grid row r, grid column c and layer l (slots ((r * 8 + c) * 2 + l) * 16 onward) hold only block rows i with i // 128 = r and (i // 16) % 2 = l, or -1. In every grid row and layer some device uses all of its slots. block_cols[s, p] lies in panel p, between p * 8 and p * 8 + 7, also for unused slots.
All inputs are finite; a program needn't handle non-finite values.
Results may differ from a plain program's by a relative error of at most 0.001.
Values may be sent and summed in bfloat16 or wider, within the bound.
A program may use at most 256 MiB of HBM per device.

v0:
```python
import jax
import jax.numpy as jnp
from jax import lax
from jax.sharding import PartitionSpec as P

NB = 256


def grid_positions(row_ids, panels, panel_width, grid_row, rows_grid, layers, per_device):
    panel_index = row_ids // panel_width
    offset = row_ids % panel_width
    local_panel = panel_index - grid_row * (panels // rows_grid)
    layer_of = panel_index // per_device % layers
    half_rows = panels // rows_grid * panel_width // layers
    within = (
        local_panel // (per_device * layers) * per_device + local_panel % per_device
    ) * panel_width + offset
    placed = layer_of * half_rows + within
    return jnp.where(row_ids >= 0, placed, layers * half_rows).astype(jnp.int32)


def shards(owned_blocks, slot_rows, block_cols):
    own_slots = owned_blocks.shape[0]
    panels = owned_blocks.shape[1]
    block_size = owned_blocks.shape[2]
    rows_grid = lax.axis_size("row")
    cols_grid = lax.axis_size("col")
    layers = lax.axis_size("layer")
    per_device = panels // (cols_grid * layers)
    panel_width = NB // panels
    tile_rows = NB // rows_grid
    slots_here = layers * per_device
    outgoing = (
        owned_blocks.reshape(own_slots, cols_grid * layers, per_device, block_size, block_size),
        block_cols.reshape(own_slots, cols_grid * layers, per_device),
        jnp.broadcast_to(slot_rows[:, None], (own_slots, cols_grid * layers)),
        jnp.broadcast_to(block_cols[:, None, :], (own_slots, cols_grid * layers, panels)),
    )
    got_blocks, got_cols, got_rows, got_every = (
        lax.all_to_all(outgoing[0], ("col", "layer"), split_axis=1, concat_axis=0, tiled=True),
        lax.all_to_all(outgoing[1], ("col", "layer"), split_axis=1, concat_axis=0, tiled=True),
        lax.all_to_all(outgoing[2], ("col", "layer"), split_axis=1, concat_axis=0, tiled=True),
        lax.all_to_all(outgoing[3], ("col", "layer"), split_axis=1, concat_axis=0, tiled=True),
    )
    got_rows = got_rows.reshape(-1)
    slot_total = got_rows.shape[0]
    got_blocks = got_blocks.reshape(slot_total, per_device, block_size, block_size)
    got_cols = got_cols.reshape(slot_total, per_device)
    got_every = got_every.reshape(slot_total, panels)
    target = grid_positions(
        got_rows, panels, panel_width, lax.axis_index("row"), rows_grid, layers, per_device
    )
    row_tile = (
        jnp.zeros((tile_rows, per_device, block_size, block_size), jnp.bfloat16)
        .at[target]
        .set(got_blocks, mode="drop")
    )
    col_tile = jnp.zeros((tile_rows, per_device), jnp.int32).at[target].set(got_cols, mode="drop")
    every_cols = jnp.zeros((tile_rows, panels), jnp.int32).at[target].set(got_every, mode="drop")
    target_cols = lax.dynamic_slice_in_dim(
        every_cols, lax.axis_index("col") * slots_here, slots_here, 1
    )
    column_tile, column_ids = (
        lax.all_to_all(row_tile, "layer", split_axis=0, concat_axis=1, tiled=True),
        lax.all_to_all(col_tile, "layer", split_axis=0, concat_axis=1, tiled=True),
    )
    column_table, column_ids = (
        lax.all_gather(column_tile, "row", axis=0, tiled=True),
        lax.all_gather(column_ids, "row", axis=0, tiled=True),
    )
    column_table = column_table.reshape(
        panels // layers, panel_width, slots_here, block_size, block_size
    )
    column_ids = column_ids.reshape(panels // layers, panel_width, slots_here)
    initial = jnp.zeros((tile_rows, slots_here, block_size, block_size), jnp.float32)
    piece_blocks = lax.all_gather(row_tile, "col", axis=1, tiled=True)
    piece_cols = lax.all_gather(col_tile, "col", axis=1, tiled=True)
    panel_count = piece_blocks.shape[1]
    panel_steps = jnp.arange(panel_count, dtype=jnp.int32)
    offsets = piece_cols % panel_width

    def one_block(block_index):
        left_blocks = lax.dynamic_slice_in_dim(piece_blocks, block_index * 8, 8, 0)
        row_offsets = lax.dynamic_slice_in_dim(offsets, block_index * 8, 8, 0)
        wanted = lax.dynamic_slice_in_dim(target_cols, block_index * 8, 8, 0)
        chosen = column_table[panel_steps[None, :], row_offsets]
        chosen_ids = column_ids[panel_steps[None, :], row_offsets]
        matched = chosen_ids == wanted[:, None, :]
        chosen = jnp.where(matched[:, :, :, None, None], chosen, jnp.zeros((), jnp.bfloat16))
        return jnp.einsum(
            "mtab,mtsbc->msac", left_blocks, chosen, preferred_element_type=jnp.float32
        )

    products = lax.map(one_block, jnp.arange(tile_rows // 8, dtype=jnp.int32))
    partial_value = initial + products.reshape(initial.shape)
    own_rows = lax.psum_scatter(partial_value, "layer", scatter_dimension=0, tiled=True)
    return own_rows.astype(jnp.bfloat16)


def solution(mesh):
    return jax.shard_map(
        shards,
        mesh=mesh,
        in_specs=(
            P(("row", "col", "layer"), None, None, None),
            P(("row", "col", "layer")),
            P(("row", "col", "layer"), None),
        ),
        out_specs=P(("row", "layer"), "col", None, None),
        check_vma=False,
    )
```

profile of v0, /device:TPU:0, one launch (start us, length us, event | category | flops | bytes accessed | tf_op | source)
XLA Modules:
  0.0 2838.5 jit_solution(2040272807180117148)
XLA Ops:
  35.6 296.6 %all-to-all-done.4 = bf16[16,16,2,128,128]{4,3,2,0,1:T(8,128)(2,1)} async-done(((bf16[16,16,2,128,128]{4,3,2,0,1:T(8,128)(2,1)}), bf16[16,16,2,128,128]{4,3,2,0,1:T(8,128)(2,1)}, u32[]{:S(2)}, u32[]{:S(2)}) %all-to-all-start.4) | async-done | bytes 16777248 | tf_op jit(solution)/shard_map/all_to_all | solution.py:40
  337.7 42.9 %scatter_fusion = bf16[128,2,128,128]{3,2,1,0:T(8,128)(2,1)} fusion(bf16[128,2,128,128]{3,2,1,0:T(8,128)(2,1)} %broadcast_in_dim.81, s32[256]{0:T(256)S(1)} %bitcast.92, bf16[256,2,128,128]{3,2,1,0:T(8,128)(2,1)} %bitcast.21), kind=kCustom, calls=%fused_computation.4 | custom fusion | bytes 50332672 | tf_op jit(solution)/shard_map/scatter | solution.py:56
  380.6 18.7 all_to_all.95
  411.2 69.9 %all-to-all-start.1 = ((s32[16,16,2]{0,2,1:T(2,128)}), s32[16,16,2]{0,2,1:T(2,128)S(1)}, u32[]{:S(2)}, u32[]{:S(2)}) async-start(s32[16,16,2]{0,2,1:T(2,128)} %bitcast.2), calls=%async_computation.1 | async-start | bytes 32768 | tf_op jit(solution)/shard_map/all_to_all | solution.py:41
  493.1 16.8 all-gather
  522.3 151.9 %all-gather.5.cloned.1.call-done = bf16[128,4,128,128]{3,2,1,0:T(8,128)(2,1)} async-done(((bf16[64,4,128,128]{3,2,1,0:T(8,128)(2,1)}), bf16[128,4,128,128]{3,2,1,0:T(8,128)(2,1)}) %all-gather.5.cloned.1.call-update) | async-done | bytes 16777232 | tf_op jit(solution)/shard_map/all_gather | solution.py:68
  674.2 1268.5 %all-gather.7.cloned.1.call-done = bf16[128,16,128,128]{3,2,1,0:T(8,128)(2,1)} async-done(((bf16[128,2,128,128]{3,2,1,0:T(8,128)(2,1)}), bf16[128,16,128,128]{3,2,1,0:T(8,128)(2,1)}) %all-gather.7.cloned.1.call-update) | async-done | bytes 67108880 | tf_op jit(solution)/shard_map/all_gather | solution.py:76
  1942.7 835.0 %while.12 = (s32[]{:T(128)}, f32[16,8,4,128,128]{4,3,2,1,0:T(8,128)}, s32[16]{0:T(128)S(1)}, s32[128,16]{1,0:T(8,128)S(1)}, s32[16,8,4]{2,1,0:T(8,128)S(1)}, /*i...) while((s32[]{:T(128)}, ...), condition=%wide.region_4.5_spmd.clone, body=%wide.region_3.4_spmd.clone.sunk | while | flops 2155873536 | bytes 98579704 | solution.py:94
  1959.6 21.6 copy.57
  1997.3 14.4 gather_fusion
  2011.7 21.6 copy.57
  2049.6 14.4 gather_fusion
  2064.0 21.6 copy.57
  2116.2 21.6 copy.57
  2153.9 14.4 gather_fusion
  2168.3 21.6 copy.57
  2206.1 14.4 gather_fusion
  2220.5 21.6 copy.57
  2258.4 14.4 gather_fusion
  2272.8 21.6 copy.57
  2310.6 14.5 gather_fusion
  2325.0 21.6 copy.57
  2377.2 21.6 copy.57
  2429.3 21.6 copy.57
  2481.6 21.6 copy.57
  2533.7 21.6 copy.57
  2571.5 14.4 gather_fusion
  2585.9 21.6 copy.57
  2638.0 21.6 copy.57
  2690.2 21.6 copy.57
  2742.4 21.6 copy.57
  2777.7 45.1 %reduce-scatter.2.cloned.1.call-done = f32[64,4,128,128]{3,2,1,0:T(8,128)} async-done(((f32[128,4,128,128]{3,2,1,0:T(8,128)}), f32[64,4,128,128]{3,2,1,0:T(8,128)}) %reduce-scatter.2.cloned.1.call-update) | async-done | bytes 16777232 | tf_op jit(solution)/shard_map/reduce_scatter | solution.py:96
  (230 shorter events, 457.7 us)
Async XLA Ops:
  7.8 21.5 all-to-all-start
  29.3 302.8 %all-to-all-start.4 = ((bf16[16,16,2,128,128]{4,3,2,0,1:T(8,128)(2,1)}), bf16[16,16,2,128,128]{4,3,2,0,1:T(8,128)(2,1)}, u32[]{:S(2)}, u32[]{:S(2)}) async-start(bf16[16,16,2,128,128]{4,3,2,0,1:T(8,128)(2,1)} %copy.39), calls=%async_computation.4 | async-start | bytes 33554432 | tf_op jit(solution)/shard_map/all_to_all | solution.py:40
  35.4 638.8 %all-gather.5.cloned.1.call-start = ((), (), s32[]{:S(2)}) async-start(), calls=%async_computation.7 | async-start | bytes 25165824 | tf_op jit(solution)/shard_map/all_gather | solution.py:68
  399.3 11.2 copy-start
  409.8 1532.9 %all-gather.7.cloned.1.call-start = ((), (), s32[]{:S(2)}) async-start(), calls=%async_computation.8 | async-start | bytes 75497472 | tf_op jit(solution)/shard_map/all_gather | solution.py:76
  411.2 76.4 %all-to-all-start.1 = ((s32[16,16,2]{0,2,1:T(2,128)}), s32[16,16,2]{0,2,1:T(2,128)S(1)}, u32[]{:S(2)}, u32[]{:S(2)}) async-start(s32[16,16,2]{0,2,1:T(2,128)} %bitcast.2), calls=%async_computation.1 | async-start | bytes 32768 | tf_op jit(solution)/shard_map/all_to_all | solution.py:41
  489.8 20.1 all-to-all-start.2
  509.9 10.1 all-to-all-start.3
  513.4 2309.4 %reduce-scatter.2.cloned.1.call-start = ((), (), s32[]{:S(2)}) async-start(), calls=%async_computation.9 | async-start | bytes 50331648 | tf_op jit(solution)/shard_map/reduce_scatter | solution.py:96
Sparse Core Ops, SparseCore 0:
  409.9 264.2 all-gather.4
  675.7 1266.9 all-gather.6
  2777.8 44.9 reduce-scatter.1
where the time goes:
time: 2850 us; the launch traced here: 2840 us
  waiting for transfers between devices  1770 us (62%)
  local copies, waits for them, and re-layouts  738 us (26%)
  matrix products  165 us (6%)
  starting transfers between devices  90.2 us (3%)
  blocking collectives  39.9 us (1%)
    all_gather x1, waiting for transfers between devices, shards(): piece_blocks = lax.all_gather(row_tile, 'col', axis=1, tiled=True)  1270 us
    gather x32, local copies, waits for them, and re-layouts, one_block(): chosen = column_table[panel_steps[None, :], row_offsets]  575 us
    all_to_all x1, waiting for transfers between devices, shards(): lax.all_to_all(outgoing[0], ('col', 'layer'), split_axis=1, concat_axis=0...  297 us
    dot_general x16, matrix products, one_block(): jnp.einsum('mtab,mtsbc->msac', left_blocks, chosen, preferred_element_typ...  165 us
    all_gather x1, waiting for transfers between devices, shards(): lax.all_gather(column_tile, 'row', axis=0, tiled=True)  152 us
    all_to_all x1, starting transfers between devices, shards(): lax.all_to_all(outgoing[1], ('col', 'layer'), split_axis=1, concat_axis=0...  69.9 us
  transfers between devices with their start and end apart: 8, of which 6 were waited for; matrix products, arithmetic and copies ran while one was open for 1% of the time, Pallas kernels for 0%

commit v1 on v0

--- a/solution.py
+++ b/solution.py
@@ -4,6 +4,24 @@
 from jax.sharding import PartitionSpec as P
 
 NB = 256
+
+
+def gather_around(shard, axis, dim):
+    ways, here, step = (lax.axis_size(axis), lax.axis_index(axis), shard.shape[dim])
+    lengths = [n * ways if d == dim else n for d, n in enumerate(shard.shape)]
+    full = lax.dynamic_update_slice_in_dim(
+        jnp.zeros(lengths, shard.dtype), shard, here * step, axis=dim
+    )
+    going_up = going_down = shard
+    for far in range(1, ways // 2 + 1):
+        going_up = lax.ppermute(going_up, axis, [(d, (d + 1) % ways) for d in range(ways)])
+        full = lax.dynamic_update_slice_in_dim(full, going_up, (here - far) % ways * step, axis=dim)
+        if 2 * far < ways:
+            going_down = lax.ppermute(going_down, axis, [(d, (d - 1) % ways) for d in range(ways)])
+            full = lax.dynamic_update_slice_in_dim(
+                full, going_down, (here + far) % ways * step, axis=dim
+            )
+    return full
 
 
 def grid_positions(row_ids, panels, panel_width, grid_row, rows_grid, layers, per_device):
@@ -73,7 +91,7 @@
     )
     column_ids = column_ids.reshape(panels // layers, panel_width, slots_here)
     initial = jnp.zeros((tile_rows, slots_here, block_size, block_size), jnp.float32)
-    piece_blocks = lax.all_gather(row_tile, "col", axis=1, tiled=True)
+    piece_blocks = gather_around(row_tile, "col", 1)
     piece_cols = lax.all_gather(col_tile, "col", axis=1, tiled=True)
     panel_count = piece_blocks.shape[1]
     panel_steps = jnp.arange(panel_count, dtype=jnp.int32)

time: 2850 us -> 2770 us (0.972)
  waiting for transfers between devices: 1770 us -> 1480 us
  local copies, waits for them, and re-layouts: 738 us -> 849 us
  starting transfers between devices: 90.2 us -> 182 us
    all_gather x1 -> x0, waiting for transfers between devices: 1270 us -> none  [shards(): piece_blocks = lax.all_gather(row_tile, 'col', axis=1, tiled=True)]
    ppermute x0 -> x7, waiting for transfers between devices: none -> 965 us  [the longest x4 914 us: gather_around(): lax.ppermute(going_up, axis, [(d, (d + 1) % ways) for d in range(ways)])]
    all_to_all x1, waiting for transfers between devices: 5.75 us -> 175 us  [shards(): lax.all_to_all(outgoing[1], ('col', 'layer'), split_axis=1, concat_axis=0...]
    all_gather x1, waiting for transfers between devices: 152 us -> 0.01 us  [shards(): lax.all_gather(column_tile, 'row', axis=0, tiled=True)]
    ppermute x0 -> x7, starting transfers between devices: none -> 116 us  [the longest x3 85.4 us: gather_around(): lax.ppermute(going_down, axis, [(d, (d - 1) % ways) for d in range(ways)])]
    dynamic_update_slice x0 -> x8, local copies, waits for them, and re-layouts: none -> 82.7 us  [the longest x4 41.4 us: gather_around(): lax.dynamic_update_slice_in_dim(full, going_up, (here - far) % ways * ste...]
  transfers between devices with their start and end apart: 8 -> 14, of which waited for: 6 -> 9; matrix products, arithmetic and copies ran while one was open for 1% -> 5% of each run, Pallas kernels for 0% -> 0%
where the time goes in v1:
time: 2770 us; the launch traced here: 2760 us
  waiting for transfers between devices  1480 us (53%)
  local copies, waits for them, and re-layouts  849 us (31%)
  starting transfers between devices  182 us (7%)
  matrix products  165 us (6%)
  blocking collectives  41.2 us (1%)
    ppermute x4, waiting for transfers between devices, gather_around(): lax.ppermute(going_up, axis, [(d, (d + 1) % ways) for d in range(ways)])  914 us
    gather x32, local copies, waits for them, and re-layouts, one_block(): chosen = column_table[panel_steps[None, :], row_offsets]  576 us
    all_to_all x1, waiting for transfers between devices, shards(): lax.all_to_all(outgoing[0], ('col', 'layer'), split_axis=1, concat_axis=0...  297 us
    all_to_all x1, waiting for transfers between devices, shards(): lax.all_to_all(outgoing[1], ('col', 'layer'), split_axis=1, concat_axis=0...  175 us
    dot_general x16, matrix products, one_block(): jnp.einsum('mtab,mtsbc->msac', left_blocks, chosen, preferred_element_typ...  165 us
    ppermute x3, starting transfers between devices, gather_around(): lax.ppermute(going_down, axis, [(d, (d - 1) % ways) for d in range(ways)])  85.4 us
  transfers between devices with their start and end apart: 14, of which 9 were waited for; matrix products, arithmetic and copies ran while one was open for 5% of the time, Pallas kernels for 0%

profile of v1, /device:TPU:0, one launch (start us, length us, event | category | flops | bytes accessed | tf_op | source)
XLA Modules:
  0.0 2757.4 jit_solution(17503473593993878914)
XLA Ops:
  35.6 296.6 %all-to-all-done.4 = bf16[16,16,2,128,128]{4,3,2,0,1:T(8,128)(2,1)} async-done(((bf16[16,16,2,128,128]{4,3,2,0,1:T(8,128)(2,1)}), bf16[16,16,2,128,128]{4,3,2,0,1:T(8,128)(2,1)}, u32[]{:S(2)}, u32[]{:S(2)}) %all-to-all-start.4) | async-done | bytes 16777248 | tf_op jit(solution)/shard_map/all_to_all | solution.py:58
  337.6 46.1 %scatter_fusion = bf16[128,2,128,128]{3,2,1,0:T(8,128)(2,1)} fusion(bf16[128,2,128,128]{3,2,1,0:T(8,128)(2,1)} %broadcast_in_dim.84, s32[256]{0:T(256)S(1)} %bitcast.92, bf16[256,2,128,128]{3,2,1,0:T(8,128)(2,1)} %bitcast.21), kind=kCustom, calls=%fused_computation.4 | custom fusion | bytes 50332672 | tf_op jit(solution)/shard_map/scatter | solution.py:74
  383.7 23.0 collective-permute-start
  406.8 45.8 %collective-permute-start.1 = (bf16[128,2,128,128]{3,2,1,0:T(8,128)(2,1)}, bf16[128,2,128,128]{3,2,1,0:T(8,128)(2,1)}, u32[]{:S(2)}, u32[]{:S(2)}) collective-permute-start(bf16[128,2,128,128]{3,2,1,0:T(8,128)(2,1)} %scatter_fusion), channel_id=1, source_target_pairs={{0,14},{2,0},{4,2},{6,4},{8,6},{10,8},{12,10},{14,12},{1,15},{3,1}... | collective-permute-start | bytes 25165832 | tf_op jit(solution)/shard_map/ppermute | solution.py:20
  452.5 314.9 %collective-permute-done = bf16[128,2,128,128]{3,2,1,0:T(8,128)(2,1)S(1)} collective-permute-done((bf16[128,2,128,128]{3,2,1,0:T(8,128)(2,1)}, bf16[128,2,128,128]{3,2,1,0:T(8,128)(2,1)S(1)}, u32[]{:S(2)}, u32[]{:S(2)}) %collective-permute-start) | collective-permute-done | bytes 8388640 | tf_op jit(solution)/shard_map/ppermute | solution.py:17
  773.1 37.8 %collective-permute-done.1 = bf16[128,2,128,128]{3,2,1,0:T(8,128)(2,1)} collective-permute-done((bf16[128,2,128,128]{3,2,1,0:T(8,128)(2,1)}, bf16[128,2,128,128]{3,2,1,0:T(8,128)(2,1)}, u32[]{:S(2)}, u32[]{:S(2)}) %collective-permute-start.1) | collective-permute-done | bytes 8388640 | tf_op jit(solution)/shard_map/ppermute | solution.py:20
  818.4 314.2 %collective-permute-done.2 = bf16[128,2,128,128]{3,2,1,0:T(8,128)(2,1)} collective-permute-done((bf16[128,2,128,128]{3,2,1,0:T(8,128)(2,1)S(1)}, bf16[128,2,128,128]{3,2,1,0:T(8,128)(2,1)}, u32[]{:S(2)}, u32[]{:S(2)}) %collective-permute-start.2) | collective-permute-done | bytes 8388640 | tf_op jit(solution)/shard_map/ppermute | solution.py:17
  1135.2 18.5 all_to_all.95
  1177.1 32.0 %collective-permute-start.5 = (bf16[128,2,128,128]{3,2,1,0:T(8,128)(2,1)}, bf16[128,2,128,128]{3,2,1,0:T(8,128)(2,1)}, u32[]{:S(2)}, u32[]{:S(2)}) collective-permute-start(bf16[128,2,128,128]{3,2,1,0:T(8,128)(2,1)} %collective-permute-done.3), channel_id=1, source_target_pairs={{0,14},{2,0},{4,2},{6,4},{8,6},{10,8},{12,10},{14,12},{1,15},{3,1}... | collective-permute-start | bytes 25165832 | tf_op jit(solution)/shard_map/ppermute | solution.py:20
  1209.1 285.1 %collective-permute-done.4 = bf16[128,2,128,128]{3,2,1,0:T(8,128)(2,1)} collective-permute-done((bf16[128,2,128,128]{3,2,1,0:T(8,128)(2,1)}, bf16[128,2,128,128]{3,2,1,0:T(8,128)(2,1)}, u32[]{:S(2)}, u32[]{:S(2)}) %collective-permute-start.4) | collective-permute-done | bytes 8388640 | tf_op jit(solution)/shard_map/ppermute | solution.py:17
  1497.4 46.4 %all-to-all-start.1 = ((s32[16,16,2]{0,2,1:T(2,128)}), s32[16,16,2]{0,2,1:T(2,128)S(1)}, u32[]{:S(2)}, u32[]{:S(2)}) async-start(s32[16,16,2]{0,2,1:T(2,128)} %bitcast.2), calls=%async_computation.1 | async-start | bytes 32768 | tf_op jit(solution)/shard_map/all_to_all | solution.py:59
  1544.6 175.3 %all-to-all-done.1 = s32[16,16,2]{0,2,1:T(2,128)S(1)} async-done(((s32[16,16,2]{0,2,1:T(2,128)}), s32[16,16,2]{0,2,1:T(2,128)S(1)}, u32[]{:S(2)}, u32[]{:S(2)}) %all-to-all-start.1) | async-done | bytes 2080 | tf_op jit(solution)/shard_map/all_to_all | solution.py:59
  1725.2 18.3 all-gather
  1755.7 21.3 broadcast_in_dim.85
  1859.7 835.9 %while.12 = (s32[]{:T(128)}, f32[16,8,4,128,128]{4,3,2,1,0:T(8,128)}, s32[16]{0:T(128)S(1)}, s32[128,16]{1,0:T(8,128)S(1)}, s32[16,8,4]{2,1,0:T(8,128)S(1)}, /*i...) while((s32[]{:T(128)}, ...), condition=%wide.region_4.5_spmd.clone, body=%wide.region_3.4_spmd.clone.sunk | while | flops 2155873536 | bytes 98579704 | solution.py:112
  1876.6 21.6 copy.57
  1928.9 21.6 copy.57
  1981.2 21.6 copy.57
  2033.4 21.6 copy.57
  2085.7 21.6 copy.57
  2137.9 21.6 copy.57
  2190.2 21.6 copy.57
  2242.6 21.6 copy.57
  2294.8 21.6 copy.57
  2347.0 21.6 copy.57
  2399.2 21.6 copy.57
  2451.5 21.6 copy.57
  2503.7 21.6 copy.57
  2555.9 21.6 copy.57
  2608.1 21.6 copy.57
  2660.4 21.6 copy.57
  2695.7 45.7 %reduce-scatter.2.cloned.1.call-done = f32[64,4,128,128]{3,2,1,0:T(8,128)} async-done(((f32[128,4,128,128]{3,2,1,0:T(8,128)}), f32[64,4,128,128]{3,2,1,0:T(8,128)}) %reduce-scatter.2.cloned.1.call-update) | async-done | bytes 16777232 | tf_op jit(solution)/shard_map/reduce_scatter | solution.py:114
  (252 shorter events, 666.2 us)
Async XLA Ops:
  7.8 21.5 all-to-all-start
  29.3 302.8 %all-to-all-start.4 = ((bf16[16,16,2,128,128]{4,3,2,0,1:T(8,128)(2,1)}), bf16[16,16,2,128,128]{4,3,2,0,1:T(8,128)(2,1)}, u32[]{:S(2)}, u32[]{:S(2)}) async-start(bf16[16,16,2,128,128]{4,3,2,0,1:T(8,128)(2,1)} %copy.39), calls=%async_computation.4 | async-start | bytes 33554432 | tf_op jit(solution)/shard_map/all_to_all | solution.py:58
  35.3 1824.4 %all-gather.4.cloned.1.call-start = ((), (), s32[]{:S(2)}) async-start(), calls=%async_computation.7 | async-start | bytes 25165824 | tf_op jit(solution)/shard_map/all_gather | solution.py:86
  383.7 383.8 %collective-permute-start = (bf16[128,2,128,128]{3,2,1,0:T(8,128)(2,1)}, bf16[128,2,128,128]{3,2,1,0:T(8,128)(2,1)S(1)}, u32[]{:S(2)}, u32[]{:S(2)}) collective-permute-start(bf16[128,2,128,128]{3,2,1,0:T(8,128)(2,1)} %scatter_fusion), channel_id=1, source_target_pairs={{0,2},{2,4},{4,6},{6,8},{8,10},{10,12},{12,14},{14,0},{1,3},{3,5},... | collective-permute-start | bytes 25165832 | tf_op jit(solution)/shard_map/ppermute | solution.py:17
  406.8 404.1 %collective-permute-start.1 = (bf16[128,2,128,128]{3,2,1,0:T(8,128)(2,1)}, bf16[128,2,128,128]{3,2,1,0:T(8,128)(2,1)}, u32[]{:S(2)}, u32[]{:S(2)}) collective-permute-start(bf16[128,2,128,128]{3,2,1,0:T(8,128)(2,1)} %scatter_fusion), channel_id=1, source_target_pairs={{0,14},{2,0},{4,2},{6,4},{8,6},{10,8},{12,10},{14,12},{1,15},{3,1}... | collective-permute-start | bytes 25165832 | tf_op jit(solution)/shard_map/ppermute | solution.py:20
  767.5 3.2 copy-start
  770.7 361.9 %collective-permute-start.2 = (bf16[128,2,128,128]{3,2,1,0:T(8,128)(2,1)S(1)}, bf16[128,2,128,128]{3,2,1,0:T(8,128)(2,1)}, u32[]{:S(2)}, u32[]{:S(2)}) collective-permute-start(bf16[128,2,128,128]{3,2,1,0:T(8,128)(2,1)S(1)} %collective-permute-done), channel_id=1, source_target_pairs={{0,2},{2,4},{4,6},{6,8},{8,10},{10,12},{12,14},{14,0},{1,3},{3,5},... | collective-permute-start | bytes 25165832 | tf_op jit(solution)/shard_map/ppermute | solution.py:17
  810.9 366.3 %collective-permute-start.3 = (bf16[128,2,128,128]{3,2,1,0:T(8,128)(2,1)}, bf16[128,2,128,128]{3,2,1,0:T(8,128)(2,1)}, u32[]{:S(2)}, u32[]{:S(2)}) collective-permute-start(bf16[128,2,128,128]{3,2,1,0:T(8,128)(2,1)} %collective-permute-done.1), channel_id=1, source_target_pairs={{0,14},{2,0},{4,2},{6,4},{8,6},{10,8},{12,10},{14,12},{1,15},{3,1}... | collective-permute-start | bytes 25165832 | tf_op jit(solution)/shard_map/ppermute | solution.py:20
  1132.6 361.6 %collective-permute-start.4 = (bf16[128,2,128,128]{3,2,1,0:T(8,128)(2,1)}, bf16[128,2,128,128]{3,2,1,0:T(8,128)(2,1)}, u32[]{:S(2)}, u32[]{:S(2)}) collective-permute-start(bf16[128,2,128,128]{3,2,1,0:T(8,128)(2,1)} %collective-permute-done.2), channel_id=1, source_target_pairs={{0,2},{2,4},{4,6},{6,8},{8,10},{10,12},{12,14},{14,0},{1,3},{3,5},... | collective-permute-start | bytes 25165832 | tf_op jit(solution)/shard_map/ppermute | solution.py:17
  1153.7 343.0 %copy-start.1 = (s32[16,32]{1,0:T(8,128)S(1)}, s32[16,32]{1,0:T(8,128)}, u32[]{:S(2)}) copy-start(s32[16,32]{1,0:T(8,128)} %param.7) | copy-start | bytes 6148
  1177.1 662.0 %collective-permute-start.5 = (bf16[128,2,128,128]{3,2,1,0:T(8,128)(2,1)}, bf16[128,2,128,128]{3,2,1,0:T(8,128)(2,1)}, u32[]{:S(2)}, u32[]{:S(2)}) collective-permute-start(bf16[128,2,128,128]{3,2,1,0:T(8,128)(2,1)} %collective-permute-done.3), channel_id=1, source_target_pairs={{0,14},{2,0},{4,2},{6,4},{8,6},{10,8},{12,10},{14,12},{1,15},{3,1}... | collective-permute-start | bytes 25165832 | tf_op jit(solution)/shard_map/ppermute | solution.py:20
  1494.2 355.2 %collective-permute-start.6 = (bf16[128,2,128,128]{3,2,1,0:T(8,128)(2,1)}, bf16[128,2,128,128]{3,2,1,0:T(8,128)(2,1)}, u32[]{:S(2)}, u32[]{:S(2)}) collective-permute-start(bf16[128,2,128,128]{3,2,1,0:T(8,128)(2,1)} %collective-permute-done.4), channel_id=1, source_target_pairs={{0,2},{2,4},{4,6},{6,8},{8,10},{10,12},{12,14},{14,0},{1,3},{3,5},... | collective-permute-start | bytes 25165832 | tf_op jit(solution)/shard_map/ppermute | solution.py:17
  1497.4 222.5 %all-to-all-start.1 = ((s32[16,16,2]{0,2,1:T(2,128)}), s32[16,16,2]{0,2,1:T(2,128)S(1)}, u32[]{:S(2)}, u32[]{:S(2)}) async-start(s32[16,16,2]{0,2,1:T(2,128)} %bitcast.2), calls=%async_computation.1 | async-start | bytes 32768 | tf_op jit(solution)/shard_map/all_to_all | solution.py:59
  1722.0 21.6 all-to-all-start.2
  1743.6 10.1 all-to-all-start.3
  1747.1 994.3 %reduce-scatter.2.cloned.1.call-start = ((), (), s32[]{:S(2)}) async-start(), calls=%async_computation.8 | async-start | bytes 50331648 | tf_op jit(solution)/shard_map/reduce_scatter | solution.py:114
Sparse Core Ops, SparseCore 0:
  1164.3 240.9 all-gather.3
  2695.8 45.5 reduce-scatter.1
